TPU v7x, 128 devices: a whole 4x4x4 slice. The times are simulated.
128 devices in a mesh: dp: 32 (over z, y_hi, x), tensor: 4 (over y_lo, core).
Axes of the slice: x: 4, y: 4 (y_hi: 2, y_lo: 2; y = y_hi * 2 + y_lo), z: 4, core: 2. Of those that a mesh axis runs over, the one named last changes fastest.
Arguments:
- tokens: bfloat16 [32, 4, 128, 2048], P('dp', 'tensor'), may hold values from -6 to 6
- doc_ids: int32 [32, 4, 128], P('dp'), may hold values from 0 to 3, never falling along the last dimension, each value on 1 to 64 neighbouring positions
- attn_gain: float32 [2048], P(('dp', 'tensor')), may hold values from 0.5 to 1.5
- forget_floor: float32 [2048], P(('dp', 'tensor')), may hold values from 0.5 to 0.98
- w_query: bfloat16 [2048, 2048], P('dp', 'tensor'), may hold values from -0.125 to 0.125
- w_forget: bfloat16 [2048, 2048], P('dp', 'tensor'), may hold values from -0.125 to 0.125
- w_value: bfloat16 [2048, 2048], P('dp', 'tensor'), may hold values from -0.125 to 0.125
- w_outgate: bfloat16 [2048, 2048], P('dp', 'tensor'), may hold values from -0.125 to 0.125
- w_output: bfloat16 [2048, 2048], P('tensor', 'dp'), may hold values from -0.125 to 0.125
- mlp_gain: float32 [2048], P(('dp', 'tensor')), may hold values from 0.5 to 1.5
- w_gate: bfloat16 [2048, 5632], P('dp', 'tensor'), may hold values from -0.125 to 0.125
- w_up: bfloat16 [2048, 5632], P('dp', 'tensor'), may hold values from -0.125 to 0.125
- w_down: bfloat16 [5632, 2048], P('tensor', 'dp'), may hold values from -0.078125 to 0.078125
- cotangent: bfloat16 [32, 4, 128, 2048], P('dp', 'tensor'), may hold values from -6 to 6
Outputs:
- layer_out: bfloat16 [32, 4, 128, 2048], P('dp', 'tensor')
- grad_tokens: float32 [32, 4, 128, 2048], P('dp', 'tensor')
- grad_attn_gain: float32 [2048], P(('dp', 'tensor'))
- grad_floor: float32 [2048], P(('dp', 'tensor'))
- grad_query: float32 [2048, 2048], P('dp', 'tensor')
- grad_forget: float32 [2048, 2048], P('dp', 'tensor')
- grad_value: float32 [2048, 2048], P('dp', 'tensor')
- grad_outgate: float32 [2048, 2048], P('dp', 'tensor')
- grad_output: float32 [2048, 2048], P('tensor', 'dp')
- grad_mlp_gain: float32 [2048], P(('dp', 'tensor'))
- grad_gate: float32 [2048, 5632], P('dp', 'tensor')
- grad_up: float32 [2048, 5632], P('dp', 'tensor')
- grad_down: float32 [5632, 2048], P('tensor', 'dp')
Inputs may be any that keep to these rules, and one draw needn't show every extreme that they name: `doc_ids`: within each row of 128 tokens the sequence numbers never fall; each sequence has 1 to 64 tokens, and the longest has exactly 64.
All inputs are finite; a program needn't handle non-finite values.
Results may differ from a plain program's by a relative error of at most 0.025.
Values may be sent and summed in bfloat16 or wider, within the bound.
No kernel may reach another device: no remote copies, remote signals or barrier semaphores. Data moves between devices by JAX's collectives and lax.ppermute only.
A program may use at most 192 MiB of HBM per device.

v0:
```python
import jax
import jax.numpy as jnp
from jax import lax
from jax.sharding import PartitionSpec as P

HK = 128
BLOCK = 64
epsilon = 1e-06


def row_scale(values):
    return lax.rsqrt(jnp.mean(values * values, axis=-1, keepdims=True) + epsilon)


def silu_slope(values):
    sigmoid_val = jax.nn.sigmoid(values)
    return sigmoid_val * (1.0 + values * (1.0 - sigmoid_val))


def matmul_plain(left, right):
    return jnp.dot(left, right, preferred_element_type=jnp.float32)


def times_trans(left, right):
    return lax.dot_general(
        left, right, (((1,), (1,)), ((), ())), preferred_element_type=jnp.float32
    )


def trans_times(left, right):
    return lax.dot_general(
        left, right, (((0,), (0,)), ((), ())), preferred_element_type=jnp.float32
    )


def recurrence(query, forget_raw, value, floor_vec, doc_row):
    length, heads_n, chan = query.shape
    forget = floor_vec + (1.0 - floor_vec) * jax.nn.sigmoid(forget_raw)
    log_forget = jnp.log(forget)
    keyed = 1.0 - forget
    block_count = length // BLOCK

    def split_blocks(arr):
        return arr.reshape(block_count, BLOCK, heads_n, chan)

    doc_blocks = doc_row.reshape(block_count, BLOCK)
    before = jnp.concatenate([jnp.full((1,), -1, jnp.int32), doc_blocks[:-1, -1]])
    position = jnp.arange(BLOCK)
    causal = position[:, None] >= position[None, :]

    @jax.checkpoint
    def block_step(recurrent_state, pieces):
        query_block, log_b, key_b, value_block, doc_b, prev_doc = pieces
        running_total = jnp.cumsum(log_b, axis=0)
        same_doc = (causal & (doc_b[:, None] == doc_b[None, :]))[:, :, None, None]
        log_gap = running_total[:, None] - running_total[None, :]
        decay = jnp.where(same_doc, jnp.exp(jnp.where(same_doc, log_gap, 0.0)), 0.0)
        scores = jnp.einsum(
            "ihk,jhk,ijhk->ijh", query_block, key_b, decay, precision=lax.Precision.HIGHEST
        )
        intra = jnp.einsum("ijh,jhv->ihv", scores, value_block, precision=lax.Precision.HIGHEST)
        carried_over = (doc_b == prev_doc).astype(jnp.float32)[:, None, None]
        across_blocks = (
            jnp.einsum(
                "bma,maf->bmf",
                query_block * jnp.exp(running_total),
                recurrent_state,
                precision=lax.Precision.HIGHEST,
            )
            * carried_over
        )
        block_finish = running_total[-1]
        end_flag = (doc_b == doc_b[-1]).astype(jnp.float32)[:, None, None]
        weighted_values = key_b * jnp.exp(block_finish[None] - running_total) * end_flag
        carry_marker = (doc_b[-1] == prev_doc).astype(jnp.float32)
        recurrent_state = recurrent_state * (
            jnp.exp(block_finish)[:, :, None] * carry_marker
        ) + jnp.einsum(
            "dmf,dmb->mfb", weighted_values, value_block, precision=lax.Precision.HIGHEST
        )
        return (recurrent_state, intra + across_blocks)

    start_state = jnp.zeros((heads_n, chan, chan), jnp.float32)
    final_state, results = lax.scan(
        block_step,
        start_state,
        (
            split_blocks(query),
            split_blocks(log_forget),
            split_blocks(keyed),
            split_blocks(value),
            doc_blocks,
            before,
        ),
    )
    return results.reshape(length, heads_n, chan)


def row_gather(values):
    count = 4
    spread = jnp.broadcast_to(values[None], (count,) + values.shape)
    got = lax.all_to_all(spread, "tensor", 0, 0, tiled=False)
    return got.reshape((-1,) + values.shape[1:])


def row_sum(values):
    count = 4
    blocks = values.reshape((count, -1) + values.shape[1:])
    got = lax.all_to_all(blocks, "tensor", 0, 0, tiled=False)
    return got.sum(axis=0)


def small_gather(vectors):
    count = 128
    spread = jnp.broadcast_to(vectors[None], (count,) + vectors.shape)
    got = lax.all_to_all(spread, ("dp", "tensor"), 0, 0, tiled=False)
    return jnp.swapaxes(got, 0, 1).reshape(vectors.shape[0], -1)


def small_sum(vectors):
    count = 128
    blocks = vectors.reshape(vectors.shape[0], count, -1)
    got = lax.all_to_all(jnp.swapaxes(blocks, 0, 1), ("dp", "tensor"), 0, 0, tiled=False)
    return got.sum(axis=0)


def shards(
    tokens,
    doc_ids,
    attn_gain,
    forget_floor,
    w_query,
    w_forget,
    w_value,
    w_outgate,
    w_output,
    mlp_gain,
    w_gate,
    w_up,
    w_down,
    cotangent,
):
    gains = small_gather(jnp.stack([attn_gain, forget_floor, mlp_gain]))
    attn_full, floor_full, mlp_full = (gains[0], gains[1], gains[2])
    part_index = lax.axis_index("tensor")
    local_width = w_query.shape[1]
    local_heads = local_width // HK
    hidden_width = w_gate.shape[1]
    floor_local = lax.dynamic_slice_in_dim(
        floor_full, part_index * local_width, local_width
    ).reshape(local_heads, HK)
    model_width = attn_full.shape[0]
    doc_all = doc_ids[0]
    row_count = doc_all.shape[0]
    resid_in = tokens[0].reshape(-1, model_width).astype(jnp.float32)
    cot_local = cotangent[0].reshape(-1, model_width)
    attn_pack = jnp.concatenate([w_query, w_forget, w_value, w_outgate, w_output.T], axis=1)
    mlp_pack = jnp.concatenate([w_gate, w_up, w_down.T], axis=1)
    attn_all = lax.all_gather(attn_pack, "dp", axis=0, tiled=True)
    mlp_all = lax.all_gather(mlp_pack, "dp", axis=0, tiled=True)
    wq_all = attn_all[:, 0 * local_width : 1 * local_width]
    wf_all = attn_all[:, 1 * local_width : 2 * local_width]
    wv_all = attn_all[:, 2 * local_width : 3 * local_width]
    wg_all = attn_all[:, 3 * local_width : 4 * local_width]
    wo_t = attn_all[:, 4 * local_width : 5 * local_width]
    wgate_all = mlp_all[:, 0:hidden_width]
    wup_all = mlp_all[:, hidden_width : 2 * hidden_width]
    wdown_t = mlp_all[:, 2 * hidden_width : 3 * hidden_width]
    scale_one = row_scale(resid_in)
    normed = row_gather((resid_in * scale_one * attn_full).astype(jnp.bfloat16))
    query = matmul_plain(normed, wq_all)
    forget_raw = matmul_plain(normed, wf_all)
    value = matmul_plain(normed, wv_all)
    out_gate = matmul_plain(normed, wg_all)

    def mixer(query_in, forget_in, value_in, floor_in):

        def shaped(arr):
            return arr.reshape(row_count, -1, local_heads, HK)

        mixed_rows = jax.vmap(recurrence, in_axes=(0, 0, 0, None, 0))(
            shaped(query_in), shaped(forget_in), shaped(value_in), floor_in, doc_all
        )
        return mixed_rows.reshape(query_in.shape[0], local_width)

    mixed, pullback = jax.vjp(mixer, query, forget_raw, value, floor_local)
    gate_act = jax.nn.silu(out_gate)
    gated = (mixed * gate_act).astype(jnp.bfloat16)
    branch = row_sum(times_trans(gated, wo_t))
    resid = resid_in + branch
    scale_two = row_scale(resid)
    normed2 = row_gather((resid * scale_two * mlp_full).astype(jnp.bfloat16))
    gate_proj = matmul_plain(normed2, wgate_all)
    up_proj = matmul_plain(normed2, wup_all)
    gate_silu = jax.nn.silu(gate_proj)
    hidden = (gate_silu * up_proj).astype(jnp.bfloat16)
    ffn_out = row_sum(times_trans(hidden, wdown_t))
    layer_out = (resid + ffn_out).astype(jnp.bfloat16).reshape(tokens.shape)
    cot_full = row_gather(cot_local)
    d_hidden = matmul_plain(cot_full, wdown_t)
    grad_down_t = trans_times(cot_full, hidden)
    d_gate = (d_hidden * up_proj * silu_slope(gate_proj)).astype(jnp.bfloat16)
    d_up = (d_hidden * gate_silu).astype(jnp.bfloat16)
    grad_gate = trans_times(normed2, d_gate)
    grad_up = trans_times(normed2, d_up)
    mlp_grads = jnp.concatenate(
        [
            grad_gate.astype(jnp.bfloat16),
            grad_up.astype(jnp.bfloat16),
            grad_down_t.astype(jnp.bfloat16),
        ],
        axis=1,
    )
    mlp_red = lax.psum_scatter(mlp_grads, "dp", scatter_dimension=0, tiled=True).astype(jnp.float32)
    d_normed2 = row_sum(times_trans(d_gate, wgate_all) + times_trans(d_up, wup_all))
    grad_mlp = jnp.sum(d_normed2 * resid * scale_two, axis=0)
    inner_two = jnp.mean(d_normed2 * mlp_full * resid, axis=-1, keepdims=True)
    d_resid = (
        cot_local.astype(jnp.float32)
        + d_normed2 * mlp_full * scale_two
        - resid * scale_two**3 * inner_two
    )
    d_branch = row_gather(d_resid.astype(jnp.bfloat16))
    d_gated = matmul_plain(d_branch, wo_t)
    grad_output_t = trans_times(d_branch, gated)
    d_mixed = d_gated * gate_act
    d_outgate = (d_gated * mixed * silu_slope(out_gate)).astype(jnp.bfloat16)
    d_query, d_forget, d_value, d_floor = pullback(d_mixed)
    d_query = d_query.astype(jnp.bfloat16)
    d_forget = d_forget.astype(jnp.bfloat16)
    d_value = d_value.astype(jnp.bfloat16)
    grad_query = trans_times(normed, d_query)
    grad_forget = trans_times(normed, d_forget)
    grad_value = trans_times(normed, d_value)
    grad_outgate = trans_times(normed, d_outgate)
    attn_grads = jnp.concatenate(
        [
            grad_query.astype(jnp.bfloat16),
            grad_forget.astype(jnp.bfloat16),
            grad_value.astype(jnp.bfloat16),
            grad_outgate.astype(jnp.bfloat16),
            grad_output_t.astype(jnp.bfloat16),
        ],
        axis=1,
    )
    attn_red = lax.psum_scatter(attn_grads, "dp", scatter_dimension=0, tiled=True).astype(
        jnp.float32
    )
    d_normed = row_sum(
        times_trans(d_query, wq_all)
        + times_trans(d_forget, wf_all)
        + times_trans(d_value, wv_all)
        + times_trans(d_outgate, wg_all)
    )
    grad_attn = jnp.sum(d_normed * resid_in * scale_one, axis=0)
    inner_one = jnp.mean(d_normed * attn_full * resid_in, axis=-1, keepdims=True)
    grad_tokens = (
        d_resid + d_normed * attn_full * scale_one - resid_in * scale_one**3 * inner_one
    ).reshape(tokens.shape)
    floor_vector = lax.dynamic_update_slice(
        jnp.zeros((model_width,), jnp.float32), d_floor.reshape(-1), (part_index * local_width,)
    )
    reduced_small = small_sum(jnp.stack([grad_attn, floor_vector, grad_mlp]))
    return (
        layer_out,
        grad_tokens,
        reduced_small[0],
        reduced_small[1],
        attn_red[:, 0 * local_width : 1 * local_width],
        attn_red[:, 1 * local_width : 2 * local_width],
        attn_red[:, 2 * local_width : 3 * local_width],
        attn_red[:, 3 * local_width : 4 * local_width],
        attn_red[:, 4 * local_width : 5 * local_width].T,
        reduced_small[2],
        mlp_red[:, 0:hidden_width],
        mlp_red[:, hidden_width : 2 * hidden_width],
        mlp_red[:, 2 * hidden_width : 3 * hidden_width].T,
    )


def solution(mesh):
    return jax.shard_map(
        shards,
        mesh=mesh,
        in_specs=(
            P("dp", "tensor", None, None),
            P("dp", None, None),
            P(("dp", "tensor")),
            P(("dp", "tensor")),
            P("dp", "tensor"),
            P("dp", "tensor"),
            P("dp", "tensor"),
            P("dp", "tensor"),
            P("tensor", "dp"),
            P(("dp", "tensor")),
            P("dp", "tensor"),
            P("dp", "tensor"),
            P("tensor", "dp"),
            P("dp", "tensor", None, None),
        ),
        out_specs=(
            P("dp", "tensor", None, None),
            P("dp", "tensor", None, None),
            P(("dp", "tensor")),
            P(("dp", "tensor")),
            P("dp", "tensor"),
            P("dp", "tensor"),
            P("dp", "tensor"),
            P("dp", "tensor"),
            P("tensor", "dp"),
            P(("dp", "tensor")),
            P("dp", "tensor"),
            P("dp", "tensor"),
            P("tensor", "dp"),
        ),
        check_vma=False,
    )
```

profile of v0, /device:TPU:0, one launch (start us, length us, event | category | flops | bytes accessed | tf_op | source)
XLA Modules:
  0.0 1291.5 jit_solution(5244657009365066844)
XLA Ops:
  15.7 11.1 all-to-all-start
  28.6 10.2 all-to-all-done
  41.7 4.5 all-to-all-start.1
  47.0 96.4 %all-gather.3.cloned.1.call-done = bf16[2048,2560]{1,0:T(8,128)(2,1)} async-done(((bf16[64,2560]{1,0:T(8,128)(2,1)}), bf16[2048,2560]{1,0:T(8,128)(2,1)}) %all-gather.3.cloned.1.call-update) | async-done | bytes 10485776 | tf_op jit(solution)/shard_map/all_gather | solution.py:159
  143.4 5.4 slice_bitcast_fusion.2
  151.2 4.8 fusion.142
  157.6 4.0 copy.290
  161.6 3.5 convolution_bitcast_fusion.4
  166.2 3.9 copy.291
  170.2 4.5 convolution_bitcast_fusion.3
  174.7 140.9 %while.40 = (s32[]{:T(128)}, f32[4,4,128,128]{3,2,1,0:T(8,128)S(1)}, f32[2,4,64,4,128]{4,2,3,1,0:T(8,128)S(1)}, f32[2,4,4,128,128]{4,3,2,1,0:T(8,128)}, f32[2,4,...) while((s32[]{:T(128)}, ...), condition=%wide.region_3.4_spmd.clone, body=%wide.region_1.3_spmd.clone.sunk | while | flops 563977216 | bytes 88180056 | solution.py:84
  177.3 21.6 %exponential_select_fusion.2 = f32[4,64,64,4,128]{4,3,2,1,0:T(4,128)} fusion(f32[4,64,4,128]{3,2,1,0:T(4,128)S(1)} %fusion.238, pred[4,64,64]{2,1,0:T(8,128)(4,1)S(1)} %compare_and_fusion.4), kind=kLoop, calls=%fused_computation.76.clone.1 | loop fusion | flops 25165824 | bytes 34095104 | tf_op jit(solution)/shard_map/jvp(vmap())/while/body/eval_jaxpr/jit(_where)/select_n | solution.py:57
  200.9 36.4 %fusion.241 = f32[4,64,64,4]{1,2,3,0:T(8,128)S(1)} fusion(f32[4,64,64,4,128]{4,3,2,1,0:T(4,128)} %exponential_select_fusion.2, f32[4,4,128,64]{2,3,1,0:T(8,128)S(1)} %copy.466, f32[4,4,128,64]{2,3,1,0:T(8,128)S(1)} %copy.468), kind=kLoop, calls=%fused_computation.75.clone.1 | loop fusion | flops 25100288 | bytes 34865152 | tf_op jit(solution)/shard_map/jvp(vmap())/while/body/eval_jaxpr/ihk,jhk,ijhk->ijh/dot_general | solution.py:58
  247.5 21.6 %exponential_select_fusion.2 = f32[4,64,64,4,128]{4,3,2,1,0:T(4,128)} fusion(f32[4,64,4,128]{3,2,1,0:T(4,128)S(1)} %fusion.238, pred[4,64,64]{2,1,0:T(8,128)(4,1)S(1)} %compare_and_fusion.4), kind=kLoop, calls=%fused_computation.76.clone.1 | loop fusion | flops 25165824 | bytes 34095104 | tf_op jit(solution)/shard_map/jvp(vmap())/while/body/eval_jaxpr/jit(_where)/select_n | solution.py:57
  271.1 36.4 %fusion.241 = f32[4,64,64,4]{1,2,3,0:T(8,128)S(1)} fusion(f32[4,64,64,4,128]{4,3,2,1,0:T(4,128)} %exponential_select_fusion.2, f32[4,4,128,64]{2,3,1,0:T(8,128)S(1)} %copy.466, f32[4,4,128,64]{2,3,1,0:T(8,128)S(1)} %copy.468), kind=kLoop, calls=%fused_computation.75.clone.1 | loop fusion | flops 25100288 | bytes 34865152 | tf_op jit(solution)/shard_map/jvp(vmap())/while/body/eval_jaxpr/ihk,jhk,ijhk->ijh/dot_general | solution.py:58
  311.9 3.3 convolution_add_fusion.5
  316.3 4.9 fusion.131
  324.3 51.7 %all_to_all.50 = f32[4,128,2048]{2,1,0:T(8,128)} all-to-all(f32[4,128,2048]{2,1,0:T(8,128)S(1)} %bitcast.501), channel_id=1, replica_groups=mesh['dp'=32,'tensor'=4] {'tensor'}, dimensions={0} | all-to-all | bytes 8388608 | tf_op jit(solution)/shard_map/all_to_all | solution.py:109
  377.6 4.6 all-to-all-start.5
  385.4 22.6 %all-to-all-done.5 = bf16[4,128,2048]{2,1,0:T(8,128)(2,1)} async-done(((bf16[4,128,2048]{2,1,0:T(8,128)(2,1)}), bf16[4,128,2048]{2,1,0:T(8,128)(2,1)}, u32[]{:S(2)}, u32[]{:S(2)}) %all-to-all-start.5) | async-done | bytes 2097184 | tf_op jit(solution)/shard_map/all_to_all | solution.py:102
  409.5 4.4 all-to-all-start.3
  414.0 8.3 fusion.77
  422.3 17.5 %all-to-all-done.3 = bf16[4,128,2048]{2,1,0:T(8,128)(2,1)} async-done(((bf16[4,128,2048]{2,1,0:T(8,128)(2,1)}), bf16[4,128,2048]{2,1,0:T(8,128)(2,1)}, u32[]{:S(2)}, u32[]{:S(2)}) %all-to-all-start.3) | async-done | bytes 2097184 | tf_op jit(solution)/shard_map/all_to_all | solution.py:102
  439.7 8.4 fusion.71
  449.8 7.8 multiply_convert_fusion.1
  457.6 5.1 fusion.69
  462.7 5.3 fusion.80
  468.0 51.6 %all_to_all.51 = f32[4,128,2048]{2,1,0:T(8,128)} all-to-all(f32[4,128,2048]{2,1,0:T(8,128)S(1)} %bitcast.513), channel_id=1, replica_groups=mesh['dp'=32,'tensor'=4] {'tensor'}, dimensions={0} | all-to-all | bytes 8388608 | tf_op jit(solution)/shard_map/all_to_all | solution.py:109
  525.2 3.6 all-to-all-start.7
  530.6 23.9 %all-to-all-done.7 = bf16[4,128,2048]{2,1,0:T(8,128)(2,1)S(1)} async-done(((bf16[4,128,2048]{2,1,0:T(8,128)(2,1)}), bf16[4,128,2048]{2,1,0:T(8,128)(2,1)S(1)}, u32[]{:S(2)}, u32[]{:S(2)}) %all-to-all-start.7) | async-done | bytes 2097184 | tf_op jit(solution)/shard_map/all_to_all | solution.py:102
  554.4 5.7 fusion.133
  565.6 183.3 %while.41 = (s32[]{:T(128)}, f32[4,4,128,128]{3,2,1,0:T(8,128)}, bf16[2,4,64,4,128]{4,2,3,1,0:T(8,128)(2,1)}, f32[2,4,64,4,128]{4,3,2,1,0:T(4,128)}, f32[2,4,64,...) while((s32[]{:T(128)}, f32[4,4,128,128]{3,2,1,0:T(8,128)}, ...), condition=%wide.region_16.17_spmd.clone, body=%wide.region_9.16_spmd.clone.sunk | while | flops 1228907520 | bytes 80963376 | solution.py:84
  577.1 4.2 convolution_add_fusion.6
  585.8 14.8 %fusion.258 = f32[4,4,128,64]{2,3,1,0:T(8,128)} fusion(f32[4,4,128,64]{2,1,3,0:T(4,128)} %copy.479, f32[4,64,4,128]{3,1,2,0:T(8,128)} %copy-done.12, f32[4,64,4,128]{3,2,1,0:T(4,128)S(1)} %fusion.257, f32[4,64,64,4]{2,3,1,0:T(4,128)} %copy.480, pred[4,64,64]{2,1,0:T(8,128)(4,1)S(1)} %compare_and_fusion.5), kind=kLoop, calls=%fused_computation.3.clone.1 | loop fusion | flops 50200576 | bytes 2375680 | tf_op jit(solution)/shard_map/transpose(jvp(vmap()))/while/body/eval_jaxpr/checkpoint/ihk,jhk,ijhk->ijh/dot_general | solution.py:58
  600.6 14.3 %fusion.259 = f32[4,4,128,64]{2,1,3,0:T(4,128)} fusion(f32[4,4,128,64]{2,3,1,0:T(8,128)S(1)} %bitcast.496, f32[4,64,4,128]{3,1,2,0:T(8,128)S(1)} %copy-done.13, f32[4,64,4,128]{3,2,1,0:T(4,128)S(1)} %fusion.257, f32[4,64,64,4]{2,3,1,0:T(4,128)S(1)} %copy-done.16, pred[4,64,64]{2,1,0:T(8,128)(4,1)S(1)} %compare_and_fusion.5), kind=kLoop, calls=%fused_computation.11.clone.1 | loop fusion | flops 50200576 | bytes 2375680 | tf_op jit(solution)/shard_map/transpose(jvp(vmap()))/while
  618.0 4.6 bitcast_dynamic-update-slice_fusion.7
  622.6 27.4 %fusion.260 = (f32[4,64,4,128]{3,1,2,0:T(8,128)S(1)}, f32[4,64,4,128]{3,2,1,0:T(4,128)}, f32[4,64,64,4]{2,3,1,0:T(4,128)S(1)}) fusion(f32[4,4,128,64]{2,3,1,0:T(8,128)S(1)} %bitcast.497, f32[4,4,128,64]{2,1,3,0:T(4,128)S(1)} %copy-done.15, f32[4,64,4,128]{3,1,2,0:T(8,128)S(1)} %copy-done.14, f32[4,64,4,128]{3,2,1,0:T(4,128)S(1)} %fusion.257, ...), kind=kLoop, calls=%fused_computation.16.clone.1 | loop fusion | flops 100335616 | bytes 3686400 | tf_op jit(solution)/shard_map/transpose(jvp(vmap()))/while/body/eval_jaxpr/checkpoint/reduce_sum | solution.py:56
  669.1 4.2 convolution_add_fusion.6
  677.8 14.8 %fusion.258 = f32[4,4,128,64]{2,3,1,0:T(8,128)} fusion(f32[4,4,128,64]{2,1,3,0:T(4,128)} %copy.479, f32[4,64,4,128]{3,1,2,0:T(8,128)} %copy-done.12, f32[4,64,4,128]{3,2,1,0:T(4,128)S(1)} %fusion.257, f32[4,64,64,4]{2,3,1,0:T(4,128)} %copy.480, pred[4,64,64]{2,1,0:T(8,128)(4,1)S(1)} %compare_and_fusion.5), kind=kLoop, calls=%fused_computation.3.clone.1 | loop fusion | flops 50200576 | bytes 2375680 | tf_op jit(solution)/shard_map/transpose(jvp(vmap()))/while/body/eval_jaxpr/checkpoint/ihk,jhk,ijhk->ijh/dot_general | solution.py:58
  692.6 14.3 %fusion.259 = f32[4,4,128,64]{2,1,3,0:T(4,128)} fusion(f32[4,4,128,64]{2,3,1,0:T(8,128)S(1)} %bitcast.496, f32[4,64,4,128]{3,1,2,0:T(8,128)S(1)} %copy-done.13, f32[4,64,4,128]{3,2,1,0:T(4,128)S(1)} %fusion.257, f32[4,64,64,4]{2,3,1,0:T(4,128)S(1)} %copy-done.16, pred[4,64,64]{2,1,0:T(8,128)(4,1)S(1)} %compare_and_fusion.5), kind=kLoop, calls=%fused_computation.11.clone.1 | loop fusion | flops 50200576 | bytes 2375680 | tf_op jit(solution)/shard_map/transpose(jvp(vmap()))/while
  709.9 4.7 bitcast_dynamic-update-slice_fusion.7
  714.6 27.4 %fusion.260 = (f32[4,64,4,128]{3,1,2,0:T(8,128)S(1)}, f32[4,64,4,128]{3,2,1,0:T(4,128)}, f32[4,64,64,4]{2,3,1,0:T(4,128)S(1)}) fusion(f32[4,4,128,64]{2,3,1,0:T(8,128)S(1)} %bitcast.497, f32[4,4,128,64]{2,1,3,0:T(4,128)S(1)} %copy-done.15, f32[4,64,4,128]{3,1,2,0:T(8,128)S(1)} %copy-done.14, f32[4,64,4,128]{3,2,1,0:T(4,128)S(1)} %fusion.257, ...), kind=kLoop, calls=%fused_computation.16.clone.1 | loop fusion | flops 100335616 | bytes 3686400 | tf_op jit(solution)/shard_map/transpose(jvp(vmap()))/while/body/eval_jaxpr/checkpoint/reduce_sum | solution.py:56
  754.5 4.2 fusion.87
  758.7 4.2 fusion.86
  762.9 4.3 fusion.85
  767.2 4.4 fusion.84
  774.3 13.8 %copy.349 = bf16[2048,2560]{1,0:T(8,128)(2,1)} copy(bf16[2048,2560]{0,1:T(8,128)(2,1)} %fusion.83) | data formatting | bytes 20971520
  788.4 5.3 convolution_convert_fusion.1
  793.7 5.0 convolution_convert_fusion.2
  798.7 4.8 fusion.64
  803.5 7.7 pad_maximum_fusion
  811.2 21.2 %copy.351 = bf16[2048,4224]{1,0:T(8,128)(2,1)} copy(bf16[2048,4224]{0,1:T(8,128)(2,1)} %pad_maximum_fusion) | data formatting | bytes 34603008
  832.4 8.7 fusion.67
  841.1 5.0 all-to-all-start.4
  854.8 5.0 add_add_fusion
  859.8 100.0 %all-to-all-done.4 = f32[4,128,2048]{2,1,0:T(8,128)} async-done(((f32[4,128,2048]{2,1,0:T(8,128)}), f32[4,128,2048]{2,1,0:T(8,128)}, u32[]{:S(2)}, u32[]{:S(2)}) %all-to-all-start.4) | async-done | bytes 4194336 | tf_op jit(solution)/shard_map/all_to_all | solution.py:109
  959.7 5.0 all-to-all-start.8
  964.9 3.6 reduce_sum.223
  970.1 51.1 %all-to-all-done.8 = f32[4,128,2048]{2,1,0:T(8,128)} async-done(((f32[4,128,2048]{2,1,0:T(8,128)}), f32[4,128,2048]{2,1,0:T(8,128)}, u32[]{:S(2)}, u32[]{:S(2)}) %all-to-all-start.8) | async-done | bytes 4194336 | tf_op jit(solution)/shard_map/all_to_all | solution.py:109
  1021.2 3.6 reduce_sum.228
  1027.4 9.2 all-to-all-start.9
  1036.6 3.5 fusion.128
  1040.1 8.6 all-to-all-done.9
  1054.7 221.6 %reduce-scatter.9.cloned.1.call-done = bf16[64,4224]{1,0:T(8,128)(2,1)} async-done(((bf16[2048,4224]{1,0:T(8,128)(2,1)}), bf16[64,4224]{1,0:T(8,128)(2,1)}) %reduce-scatter.9.cloned.1.call-update) | async-done | bytes 540688
  (361 shorter events, 151.8 us)
Async XLA Ops:
  7.2 32.8 %copy-start.7 = (bf16[1,1,128,2048]{3,2,1,0:T(8,128)(2,1)S(1)}, bf16[1,1,128,2048]{3,2,1,0:T(8,128)(2,1)}, u32[]{:S(2)}) copy-start(bf16[1,1,128,2048]{3,2,1,0:T(8,128)(2,1)} %param.18) | copy-start | bytes 1572868
  7.2 136.2 %all-gather.3.cloned.1.call-start = ((), (), s32[]{:S(2)}) async-start(), calls=%async_computation.12 | async-start | bytes 10813440 | tf_op jit(solution)/shard_map/all_gather | solution.py:159
  12.3 401.7 %all-gather.5.cloned.1.call-start = ((), (), s32[]{:S(2)}) async-start(), calls=%async_computation.13 | async-start | bytes 17842176 | tf_op jit(solution)/shard_map/all_gather | solution.py:160
  15.7 23.1 %all-to-all-start = ((f32[128,3,16]{2,1,0:T(4,128)}), f32[128,3,16]{2,1,0:T(4,128)S(1)}, u32[]{:S(2)}, u32[]{:S(2)}) async-start(f32[128,3,16]{2,1,0:T(4,128)} %broadcast_in_dim.179), calls=%async_computation | async-start | bytes 524288 | tf_op jit(solution)/shard_map/all_to_all | solution.py:116
  28.1 18.1 %copy-start.52 = (s32[1,4,128]{2,1,0:T(4,128)S(1)}, s32[1,4,128]{2,1,0:T(4,128)}, u32[]{:S(2)}) copy-start(s32[1,4,128]{2,1,0:T(4,128)} %param.19) | copy-start | bytes 6148
  28.6 13.1 %copy-start.50 = (f32[128]{0:T(128)}, f32[128]{0:T(128)S(1)}, u32[]{:S(2)}) copy-start(f32[128]{0:T(128)S(1)} %get-tuple-element.863) | copy-start | bytes 1540
  41.7 109.5 %all-to-all-start.1 = ((bf16[4,128,2048]{2,1,0:T(8,128)(2,1)}), bf16[4,128,2048]{2,1,0:T(8,128)(2,1)}, u32[]{:S(2)}, u32[]{:S(2)}) async-start(bf16[4,128,2048]{2,1,0:T(8,128)(2,1)} %broadcast_in_dim.180), calls=%async_computation.1 | async-start | bytes 4194304 | tf_op jit(solution)/shard_map/all_to_all | solution.py:102
  47.0 104.2 %copy-start.44 = (f32[4,128]{1,0:T(4,128)}, f32[4,128]{1,0:T(4,128)S(1)}, u32[]{:S(2)}) copy-start(f32[4,128]{1,0:T(4,128)S(1)} %get-tuple-element.828) | copy-start | bytes 6148
  47.0 104.2 %copy-start.46 = (f32[4,128]{1,0:T(4,128)}, f32[4,128]{1,0:T(4,128)S(1)}, u32[]{:S(2)}) copy-start(f32[4,128]{1,0:T(4,128)S(1)} %get-tuple-element.829) | copy-start | bytes 6148
  315.6 5.6 copy-start.18
  316.3 4.9 copy-start.35
  324.3 51.7 %copy-start.21 = (bf16[1,1,128,2048]{3,2,1,0:T(8,128)(2,1)S(1)}, bf16[1,1,128,2048]{3,2,1,0:T(8,128)(2,1)}, u32[]{:S(2)}) copy-start(bf16[1,1,128,2048]{3,2,1,0:T(8,128)(2,1)} %param.31) | copy-start | bytes 1572868
  376.1 6.2 copy-start.38
  377.6 7.3 copy-start.8
  377.6 30.3 %all-to-all-start.5 = ((bf16[4,128,2048]{2,1,0:T(8,128)(2,1)}), bf16[4,128,2048]{2,1,0:T(8,128)(2,1)}, u32[]{:S(2)}, u32[]{:S(2)}) async-start(bf16[4,128,2048]{2,1,0:T(8,128)(2,1)} %broadcast_in_dim.183), calls=%async_computation.5 | async-start | bytes 4194304 | tf_op jit(solution)/shard_map/all_to_all | solution.py:102
  382.3 140.8 %copy-start.39 = (f32[2048]{0:T(1024)}, f32[2048]{0:T(1024)S(1)}, u32[]{:S(2)}) copy-start(f32[2048]{0:T(1024)S(1)} %mul.610) | copy-start | bytes 24580
  384.9 138.2 %copy-start.5 = (f32[128,2048]{1,0:T(8,128)}, f32[128,2048]{1,0:T(8,128)S(1)}, u32[]{:S(2)}) copy-start(f32[128,2048]{1,0:T(8,128)S(1)} %reduce_sum.220) | copy-start | bytes 3145732
  385.2 138.0 %copy-start.48 = (f32[128]{0:T(128)}, f32[128]{0:T(128)S(1)}, u32[]{:S(2)}) copy-start(f32[128]{0:T(128)S(1)} %get-tuple-element.865) | copy-start | bytes 1540
  385.2 138.0 %copy-start.53 = (f32[128]{0:T(128)}, f32[128]{0:T(128)S(1)}, u32[]{:S(2)}) copy-start(f32[128]{0:T(128)S(1)} %get-tuple-element.864) | copy-start | bytes 1540
  409.5 30.2 %all-to-all-start.3 = ((bf16[4,128,2048]{2,1,0:T(8,128)(2,1)}), bf16[4,128,2048]{2,1,0:T(8,128)(2,1)}, u32[]{:S(2)}, u32[]{:S(2)}) async-start(bf16[4,128,2048]{2,1,0:T(8,128)(2,1)} %broadcast_in_dim.181), calls=%async_computation.3 | async-start | bytes 4194304 | tf_op jit(solution)/shard_map/all_to_all | solution.py:102
  439.7 9.1 copy-start.58
  439.7 10.1 copy-start.63
  457.6 5.1 copy-start.62
  457.6 5.1 copy-start.59
  525.2 29.3 %all-to-all-start.7 = ((bf16[4,128,2048]{2,1,0:T(8,128)(2,1)}), bf16[4,128,2048]{2,1,0:T(8,128)(2,1)S(1)}, u32[]{:S(2)}, u32[]{:S(2)}) async-start(bf16[4,128,2048]{2,1,0:T(8,128)(2,1)} %broadcast_in_dim.184), calls=%async_computation.7 | async-start | bytes 4194304 | tf_op jit(solution)/shard_map/all_to_all | solution.py:102
  528.8 520.6 %reduce-scatter.7.cloned.1.call-start = ((), (), s32[]{:S(2)}) async-start(), calls=%async_computation.14 | async-start | bytes 10813440
  554.4 5.7 copy-start.27
  554.4 7.3 copy-start.19
  560.1 5.4 copy-start.32
  577.1 6.3 copy-start.3
  585.8 14.8 %copy-start = (f32[4,64,4,128]{3,1,2,0:T(8,128)S(1)}, f32[4,64,4,128]{3,1,2,0:T(8,128)}, u32[]{:S(2)}) copy-start(f32[4,64,4,128]{3,1,2,0:T(8,128)} %dynamic-slice_bitcast_fusion.20) | copy-start | bytes 1572868 | tf_op jit(solution)/shard_map/transpose(jvp(vmap()))/while
  585.8 14.8 %copy-start.13 = (f32[4,64,4,128]{3,1,2,0:T(8,128)S(1)}, f32[4,64,4,128]{3,1,2,0:T(8,128)}, u32[]{:S(2)}) copy-start(f32[4,64,4,128]{3,1,2,0:T(8,128)} %copy-done.12) | copy-start | bytes 1572868 | tf_op jit(solution)/shard_map/transpose(jvp(vmap()))/while
  585.8 14.8 %copy-start.16 = (f32[4,64,64,4]{2,3,1,0:T(4,128)S(1)}, f32[4,64,64,4]{2,3,1,0:T(4,128)}, u32[]{:S(2)}) copy-start(f32[4,64,64,4]{2,3,1,0:T(4,128)} %copy.480) | copy-start | bytes 786436 | tf_op jit(solution)/shard_map/transpose(jvp(vmap()))/while
  622.6 28.1 %copy-start.2 = (f32[4,64,4,128]{3,1,2,0:T(8,128)S(1)}, f32[4,64,4,128]{3,1,2,0:T(8,128)}, u32[]{:S(2)}) copy-start(f32[4,64,4,128]{3,1,2,0:T(8,128)} %dynamic-slice_bitcast_fusion.18) | copy-start | bytes 1572868 | tf_op jit(solution)/shard_map/transpose(jvp(vmap()))/while
  622.6 28.1 %copy-start.4 = (f32[4,64,4,128]{3,1,2,0:T(8,128)S(1)}, f32[4,64,4,128]{3,1,2,0:T(8,128)}, u32[]{:S(2)}) copy-start(f32[4,64,4,128]{3,1,2,0:T(8,128)} %convolution_bitcast_fusion.10) | copy-start | bytes 1572868 | tf_op jit(solution)/shard_map/transpose(jvp(vmap()))/while
  669.1 6.3 copy-start.3
  677.7 14.8 %copy-start = (f32[4,64,4,128]{3,1,2,0:T(8,128)S(1)}, f32[4,64,4,128]{3,1,2,0:T(8,128)}, u32[]{:S(2)}) copy-start(f32[4,64,4,128]{3,1,2,0:T(8,128)} %dynamic-slice_bitcast_fusion.20) | copy-start | bytes 1572868 | tf_op jit(solution)/shard_map/transpose(jvp(vmap()))/while
  677.7 14.8 %copy-start.13 = (f32[4,64,4,128]{3,1,2,0:T(8,128)S(1)}, f32[4,64,4,128]{3,1,2,0:T(8,128)}, u32[]{:S(2)}) copy-start(f32[4,64,4,128]{3,1,2,0:T(8,128)} %copy-done.12) | copy-start | bytes 1572868 | tf_op jit(solution)/shard_map/transpose(jvp(vmap()))/while
  677.7 14.8 %copy-start.16 = (f32[4,64,64,4]{2,3,1,0:T(4,128)S(1)}, f32[4,64,64,4]{2,3,1,0:T(4,128)}, u32[]{:S(2)}) copy-start(f32[4,64,64,4]{2,3,1,0:T(4,128)} %copy.480) | copy-start | bytes 786436 | tf_op jit(solution)/shard_map/transpose(jvp(vmap()))/while
  709.9 4.7 copy-start.1
  709.9 4.7 copy-start.14
  709.9 4.7 copy-start.15
  709.9 4.7 copy-start.17
  714.6 28.1 %copy-start.2 = (f32[4,64,4,128]{3,1,2,0:T(8,128)S(1)}, f32[4,64,4,128]{3,1,2,0:T(8,128)}, u32[]{:S(2)}) copy-start(f32[4,64,4,128]{3,1,2,0:T(8,128)} %dynamic-slice_bitcast_fusion.18) | copy-start | bytes 1572868 | tf_op jit(solution)/shard_map/transpose(jvp(vmap()))/while
  714.6 28.1 %copy-start.4 = (f32[4,64,4,128]{3,1,2,0:T(8,128)S(1)}, f32[4,64,4,128]{3,1,2,0:T(8,128)}, u32[]{:S(2)}) copy-start(f32[4,64,4,128]{3,1,2,0:T(8,128)} %convolution_bitcast_fusion.10) | copy-start | bytes 1572868 | tf_op jit(solution)/shard_map/transpose(jvp(vmap()))/while
  748.8 4.7 copy-start.26
  788.1 488.2 %reduce-scatter.9.cloned.1.call-start = ((), (), s32[]{:S(2)}) async-start(), calls=%async_computation.15 | async-start | bytes 17842176
  788.3 5.3 copy-start.60
  793.7 5.0 copy-start.61
  841.1 118.7 %all-to-all-start.4 = ((f32[4,128,2048]{2,1,0:T(8,128)}), f32[4,128,2048]{2,1,0:T(8,128)}, u32[]{:S(2)}, u32[]{:S(2)}) async-start(f32[4,128,2048]{2,1,0:T(8,128)} %bitcast.512), calls=%async_computation.4 | async-start | bytes 8388608 | tf_op jit(solution)/shard_map/all_to_all | solution.py:109
  959.7 5.0 copy-start.43
  959.7 61.5 %all-to-all-start.8 = ((f32[4,128,2048]{2,1,0:T(8,128)}), f32[4,128,2048]{2,1,0:T(8,128)}, u32[]{:S(2)}, u32[]{:S(2)}) async-start(f32[4,128,2048]{2,1,0:T(8,128)} %bitcast.502), calls=%async_computation.8 | async-start | bytes 8388608 | tf_op jit(solution)/shard_map/all_to_all | solution.py:109
  964.8 60.0 %copy-start.9 = (bf16[1,1,128,2048]{3,2,1,0:T(8,128)(2,1)S(1)}, bf16[1,1,128,2048]{3,2,1,0:T(8,128)(2,1)}, u32[]{:S(2)}) copy-start(bf16[1,1,128,2048]{3,2,1,0:T(8,128)(2,1)} %param.18) | copy-start | bytes 1572868
  964.9 60.0 %copy-start.42 = (f32[2048]{0:T(1024)S(1)}, f32[2048]{0:T(1024)}, u32[]{:S(2)}) copy-start(f32[2048]{0:T(1024)} %copy-done.41) | copy-start | bytes 24580
  964.9 60.0 %copy-start.51 = (f32[128]{0:T(128)S(1)}, f32[128]{0:T(128)}, u32[]{:S(2)}) copy-start(f32[128]{0:T(128)} %copy-done.50) | copy-start | bytes 1540
  968.5 68.0 %copy-start.6 = (f32[128,2048]{1,0:T(8,128)S(1)}, f32[128,2048]{1,0:T(8,128)}, u32[]{:S(2)}) copy-start(f32[128,2048]{1,0:T(8,128)} %copy-done.5) | copy-start | bytes 3145732
  968.5 68.0 %copy-start.11 = (f32[128,2048]{1,0:T(8,128)S(1)}, f32[128,2048]{1,0:T(8,128)}, u32[]{:S(2)}) copy-start(f32[128,2048]{1,0:T(8,128)} %copy-done.10) | copy-start | bytes 3145732
  968.5 68.0 %copy-start.22 = (bf16[1,1,128,2048]{3,2,1,0:T(8,128)(2,1)S(1)}, bf16[1,1,128,2048]{3,2,1,0:T(8,128)(2,1)}, u32[]{:S(2)}) copy-start(bf16[1,1,128,2048]{3,2,1,0:T(8,128)(2,1)} %param.31) | copy-start | bytes 1572868
  968.6 68.0 %copy-start.40 = (f32[2048]{0:T(1024)S(1)}, f32[2048]{0:T(1024)}, u32[]{:S(2)}) copy-start(f32[2048]{0:T(1024)} %copy-done.39) | copy-start | bytes 24580
  968.6 68.0 %copy-start.49 = (f32[128]{0:T(128)S(1)}, f32[128]{0:T(128)}, u32[]{:S(2)}) copy-start(f32[128]{0:T(128)} %copy-done.48) | copy-start | bytes 1540
  968.6 68.0 %copy-start.54 = (f32[128]{0:T(128)S(1)}, f32[128]{0:T(128)}, u32[]{:S(2)}) copy-start(f32[128]{0:T(128)} %copy-done.53) | copy-start | bytes 1540
  968.6 68.0 %copy-start.56 = (f32[128]{0:T(128)S(1)}, f32[128]{0:T(128)}, u32[]{:S(2)}) copy-start(f32[128]{0:T(128)} %copy-done.55) | copy-start | bytes 1540
  968.6 68.0 %copy-start.57 = (f32[128]{0:T(128)S(1)}, f32[128]{0:T(128)}, u32[]{:S(2)}) copy-start(f32[128]{0:T(128)} %get-tuple-element.862) | copy-start | bytes 1540
  1027.4 21.3 %all-to-all-start.9 = ((f32[128,3,16]{2,1,0:T(4,128)}), f32[128,3,16]{2,1,0:T(4,128)S(1)}, u32[]{:S(2)}, u32[]{:S(2)}) async-start(f32[128,3,16]{2,1,0:T(4,128)} %copy.307), calls=%async_computation.9 | async-start | bytes 524288 | tf_op jit(solution)/shard_map/all_to_all | solution.py:123
  (27 other events, 77.6 us)
Sparse Core Ops, SparseCore 0:
  12.4 130.9 all-gather.2
  147.0 156.2 all-gather.4
  788.2 207.1 reduce-scatter.6
  1001.1 275.1 reduce-scatter.8
where the time goes:
time: 1300 us; the launch traced here: 1290 us
  waiting for transfers between devices  552 us (42%)
  other arithmetic  280 us (22%)
  matrix products  161 us (12%)
  local copies, waits for them, and re-layouts  130 us (10%)
  blocking collectives  103 us (8%)
  starting transfers between devices  47.8 us (4%)
  between operations  14.8 us (1%)
    unnamed x6, waiting for transfers between devices  222 us
    all_to_all x2, waiting for transfers between devices, row_sum(): got = lax.all_to_all(blocks, 'tensor', 0, 0, tiled=False)  151 us
    all_to_all x2, blocking collectives, row_sum(): got = lax.all_to_all(blocks, 'tensor', 0, 0, tiled=False)  103 us
    dot_general x4, other arithmetic, block_step(): jnp.einsum('ihk,jhk,ijhk->ijh', query_block, key_b, decay, precision=lax....  102 us
    all_gather x1, waiting for transfers between devices, shards(): attn_all = lax.all_gather(attn_pack, 'dp', axis=0, tiled=True)  96.4 us
    all_to_all x4, waiting for transfers between devices, row_gather(): got = lax.all_to_all(spread, 'tensor', 0, 0, tiled=False)  64 us
    unnamed x118, local copies, waits for them, and re-layouts  56.3 us
    reduce_sum x2, other arithmetic, block_step(): log_gap = running_total[:, None] - running_total[None, :]  54.8 us
  transfers between devices with their start and end apart: 12, of which 9 were waited for; matrix products, arithmetic and copies ran while one was open for 23% of the time, Pallas kernels for 0%

commit v1 on v0

--- a/solution.py
+++ b/solution.py
@@ -156,8 +156,12 @@
     cot_local = cotangent[0].reshape(-1, model_width)
     attn_pack = jnp.concatenate([w_query, w_forget, w_value, w_outgate, w_output.T], axis=1)
     mlp_pack = jnp.concatenate([w_gate, w_up, w_down.T], axis=1)
-    attn_all = lax.all_gather(attn_pack, "dp", axis=0, tiled=True)
-    mlp_all = lax.all_gather(mlp_pack, "dp", axis=0, tiled=True)
+    keep_up_the_numbers = lambda x_part, in_array: jnp.split(
+        lax.all_gather(jnp.concatenate([x_part, in_array], axis=1), "dp", axis=0, tiled=True),
+        [x_part.shape[1]],
+        axis=1,
+    )
+    attn_all, mlp_all = keep_up_the_numbers(attn_pack, mlp_pack)
     wq_all = attn_all[:, 0 * local_width : 1 * local_width]
     wf_all = attn_all[:, 1 * local_width : 2 * local_width]
     wv_all = attn_all[:, 2 * local_width : 3 * local_width]

time: 1300 us -> 1410 us (1.085)
  waiting for transfers between devices: 552 us -> 662 us
    all_gather x2 -> x1, waiting for transfers between devices: 96.4 us -> 206 us  [shards(): lax.all_gather(jnp.concatenate([x_part, in_array], axis=1), 'dp', axis=0,...]
    unnamed x118 -> x119, local copies, waits for them, and re-layouts: 56.3 us -> 55.4 us
    unnamed x6 -> x5, waiting for transfers between devices: 222 us -> 222 us
  transfers between devices with their start and end apart: 12 -> 11, of which waited for: 9 -> 9; matrix products, arithmetic and copies ran while one was open for 23% -> 8% of each run, Pallas kernels for 0% -> 0%
where the time goes in v1:
time: 1410 us; the launch traced here: 1400 us
  waiting for transfers between devices  662 us (47%)
  other arithmetic  276 us (20%)
  matrix products  160 us (11%)
  local copies, waits for them, and re-layouts  127 us (9%)
  blocking collectives  103 us (7%)
  starting transfers between devices  55.7 us (4%)
  between operations  15 us (1%)
    unnamed x5, waiting for transfers between devices  222 us
    all_gather x1, waiting for transfers between devices, shards(): lax.all_gather(jnp.concatenate([x_part, in_array], axis=1), 'dp', axis=0,...  206 us
    all_to_all x2, waiting for transfers between devices, row_sum(): got = lax.all_to_all(blocks, 'tensor', 0, 0, tiled=False)  151 us
    all_to_all x2, blocking collectives, row_sum(): got = lax.all_to_all(blocks, 'tensor', 0, 0, tiled=False)  103 us
    dot_general x4, other arithmetic, block_step(): jnp.einsum('ihk,jhk,ijhk->ijh', query_block, key_b, decay, precision=lax....  97.7 us
    all_to_all x4, waiting for transfers between devices, row_gather(): got = lax.all_to_all(spread, 'tensor', 0, 0, tiled=False)  63.7 us
    unnamed x119, local copies, waits for them, and re-layouts  55.4 us
    reduce_sum x2, other arithmetic, block_step(): log_gap = running_total[:, None] - running_total[None, :]  54.9 us
  transfers between devices with their start and end apart: 11, of which 9 were waited for; matrix products, arithmetic and copies ran while one was open for 8% of the time, Pallas kernels for 0%

profile of v1, /device:TPU:0, one launch (start us, length us, event | category | flops | bytes accessed | tf_op | source)
XLA Modules:
  0.0 1401.8 jit_solution(2963031015578030751)
XLA Ops:
  16.7 11.1 all-to-all-start
  29.7 10.0 all-to-all-done
  42.6 4.5 all-to-all-start.1
  47.9 206.3 %all-gather.2.cloned.1.call-done = bf16[2048,6784]{1,0:T(8,128)(2,1)} async-done(((bf16[64,6784]{1,0:T(8,128)(2,1)}), bf16[2048,6784]{1,0:T(8,128)(2,1)}) %all-gather.2.cloned.1.call-update) | async-done | bytes 27787280 | tf_op jit(solution)/shard_map/all_gather | solution.py:160
  254.2 5.3 slice_bitcast_fusion.2
  259.5 4.0 copy.286
  263.5 5.2 fusion.142
  270.3 4.0 copy.290
  274.2 3.5 convolution_bitcast_fusion.4
  281.3 4.5 convolution_bitcast_fusion.3
  286.8 144.1 %while.40 = (s32[]{:T(128)}, f32[4,4,128,128]{3,2,1,0:T(8,128)S(1)}, f32[2,4,64,4,128]{4,2,3,1,0:T(8,128)}, f32[2,4,4,128,128]{4,3,2,1,0:T(8,128)}, f32[2,4,64,4...) while((s32[]{:T(128)}, ...), condition=%wide.region_3.4_spmd.clone, body=%wide.region_1.3_spmd.clone.sunk | while | flops 563977216 | bytes 88181552 | solution.py:84
  288.4 21.6 %exponential_select_fusion.2 = f32[4,64,64,4,128]{4,3,2,1,0:T(4,128)} fusion(f32[4,64,4,128]{3,2,1,0:T(4,128)S(1)} %fusion.238, pred[4,64,64]{2,1,0:T(8,128)(4,1)S(1)} %compare_and_fusion.4), kind=kLoop, calls=%fused_computation.76.clone.1 | loop fusion | flops 25165824 | bytes 34095104 | tf_op jit(solution)/shard_map/jvp(vmap())/while/body/eval_jaxpr/jit(_where)/select_n | solution.py:57
  313.0 36.4 %fusion.241 = f32[4,64,64,4]{1,2,3,0:T(8,128)S(1)} fusion(f32[4,64,64,4,128]{4,3,2,1,0:T(4,128)} %exponential_select_fusion.2, f32[4,4,128,64]{2,3,1,0:T(8,128)S(1)} %copy.466, f32[4,4,128,64]{2,3,1,0:T(8,128)S(1)} %copy.468), kind=kLoop, calls=%fused_computation.75.clone.1 | loop fusion | flops 25100288 | bytes 34865152 | tf_op jit(solution)/shard_map/jvp(vmap())/while/body/eval_jaxpr/ihk,jhk,ijhk->ijh/dot_general | solution.py:58
  355.7 3.3 convolution_add_fusion.5
  360.4 21.6 %exponential_select_fusion.2 = f32[4,64,64,4,128]{4,3,2,1,0:T(4,128)} fusion(f32[4,64,4,128]{3,2,1,0:T(4,128)S(1)} %fusion.238, pred[4,64,64]{2,1,0:T(8,128)(4,1)S(1)} %compare_and_fusion.4), kind=kLoop, calls=%fused_computation.76.clone.1 | loop fusion | flops 25165824 | bytes 34095104 | tf_op jit(solution)/shard_map/jvp(vmap())/while/body/eval_jaxpr/jit(_where)/select_n | solution.py:57
  385.0 36.4 %fusion.241 = f32[4,64,64,4]{1,2,3,0:T(8,128)S(1)} fusion(f32[4,64,64,4,128]{4,3,2,1,0:T(4,128)} %exponential_select_fusion.2, f32[4,4,128,64]{2,3,1,0:T(8,128)S(1)} %copy.466, f32[4,4,128,64]{2,3,1,0:T(8,128)S(1)} %copy.468), kind=kLoop, calls=%fused_computation.75.clone.1 | loop fusion | flops 25100288 | bytes 34865152 | tf_op jit(solution)/shard_map/jvp(vmap())/while/body/eval_jaxpr/ihk,jhk,ijhk->ijh/dot_general | solution.py:58
  427.6 3.3 convolution_add_fusion.5
  432.8 4.9 fusion.131
  437.8 3.1 fusion.93
  440.9 51.7 %all_to_all.50 = f32[4,128,2048]{2,1,0:T(8,128)} all-to-all(f32[4,128,2048]{2,1,0:T(8,128)S(1)} %bitcast.502), channel_id=1, replica_groups=mesh['dp'=32,'tensor'=4] {'tensor'}, dimensions={0} | all-to-all | bytes 8388608 | tf_op jit(solution)/shard_map/all_to_all | solution.py:109
  494.2 4.6 all-to-all-start.5
  501.9 22.6 %all-to-all-done.5 = bf16[4,128,2048]{2,1,0:T(8,128)(2,1)} async-done(((bf16[4,128,2048]{2,1,0:T(8,128)(2,1)}), bf16[4,128,2048]{2,1,0:T(8,128)(2,1)}, u32[]{:S(2)}, u32[]{:S(2)}) %all-to-all-start.5) | async-done | bytes 2097184 | tf_op jit(solution)/shard_map/all_to_all | solution.py:102
  526.1 13.7 all-to-all-start.3
  539.8 8.2 fusion.77
  548.1 17.3 %all-to-all-done.3 = bf16[4,128,2048]{2,1,0:T(8,128)(2,1)} async-done(((bf16[4,128,2048]{2,1,0:T(8,128)(2,1)}), bf16[4,128,2048]{2,1,0:T(8,128)(2,1)}, u32[]{:S(2)}, u32[]{:S(2)}) %all-to-all-start.3) | async-done | bytes 2097184 | tf_op jit(solution)/shard_map/all_to_all | solution.py:102
  565.3 6.5 fusion.71
  571.9 8.9 multiply_convert_fusion.1
  580.8 6.5 fusion.69
  587.4 5.6 fusion.80
  592.9 51.6 %all_to_all.51 = f32[4,128,2048]{2,1,0:T(8,128)} all-to-all(f32[4,128,2048]{2,1,0:T(8,128)S(1)} %bitcast.512), channel_id=1, replica_groups=mesh['dp'=32,'tensor'=4] {'tensor'}, dimensions={0} | all-to-all | bytes 8388608 | tf_op jit(solution)/shard_map/all_to_all | solution.py:109
  650.1 3.6 all-to-all-start.7
  655.5 23.9 %all-to-all-done.7 = bf16[4,128,2048]{2,1,0:T(8,128)(2,1)S(1)} async-done(((bf16[4,128,2048]{2,1,0:T(8,128)(2,1)}), bf16[4,128,2048]{2,1,0:T(8,128)(2,1)S(1)}, u32[]{:S(2)}, u32[]{:S(2)}) %all-to-all-start.7) | async-done | bytes 2097184 | tf_op jit(solution)/shard_map/all_to_all | solution.py:102
  679.4 5.3 fusion.133
  690.2 174.0 %while.41 = (s32[]{:T(128)}, f32[4,4,128,128]{3,2,1,0:T(8,128)}, bf16[2,4,64,4,128]{4,2,3,1,0:T(8,128)(2,1)}, f32[2,4,64,4,128]{4,3,2,1,0:T(4,128)}, f32[2,4,64,...) while((s32[]{:T(128)}, f32[4,4,128,128]{3,2,1,0:T(8,128)}, ...), condition=%wide.region_16.17_spmd.clone, body=%wide.region_9.16_spmd.clone.sunk | while | flops 1228907520 | bytes 93546408 | solution.py:84
  703.7 27.5 %fusion.260 = (f32[4,64,4,128]{3,1,2,0:T(8,128)}, f32[4,64,4,128]{3,2,1,0:T(4,128)}, f32[4,64,64,4]{2,3,1,0:T(4,128)S(1)}) fusion(f32[4,4,128,64]{2,3,1,0:T(8,128)S(1)} %bitcast.499, f32[4,4,128,64]{2,1,3,0:T(4,128)S(1)} %copy.479, f32[4,64,4,128]{3,1,2,0:T(8,128)S(1)} %copy.477, f32[4,64,4,128]{3,2,1,0:T(4,128)S(1)} %fusion.257, ...), kind=kLoop, calls=%fused_computation.16.clone.1 | loop fusion | flops 100335616 | bytes 3686400 | tf_op jit(solution)/shard_map/transpose(jvp(vmap()))/while/body/eval_jaxpr/checkpoint/reduce_sum | solution.py:56
  739.3 15.5 %fusion.259 = f32[4,4,128,64]{2,1,3,0:T(4,128)S(1)} fusion(f32[4,4,128,64]{2,3,1,0:T(8,128)} %bitcast.498, f32[4,64,4,128]{3,1,2,0:T(8,128)} %copy-done.12, f32[4,64,4,128]{3,2,1,0:T(4,128)S(1)} %fusion.257, f32[4,64,64,4]{2,3,1,0:T(4,128)} %copy-done.14, pred[4,64,64]{2,1,0:T(8,128)(4,1)S(1)} %compare_and_fusion.5), kind=kLoop, calls=%fused_computation.11.clone.1 | loop fusion | flops 50200576 | bytes 2375680 | tf_op jit(solution)/shard_map/transpose(jvp(vmap()))/while
  754.8 12.5 fusion.258
  773.6 3.0 convolution_add_fusion.6
  791.1 27.5 %fusion.260 = (f32[4,64,4,128]{3,1,2,0:T(8,128)}, f32[4,64,4,128]{3,2,1,0:T(4,128)}, f32[4,64,64,4]{2,3,1,0:T(4,128)S(1)}) fusion(f32[4,4,128,64]{2,3,1,0:T(8,128)S(1)} %bitcast.499, f32[4,4,128,64]{2,1,3,0:T(4,128)S(1)} %copy.479, f32[4,64,4,128]{3,1,2,0:T(8,128)S(1)} %copy.477, f32[4,64,4,128]{3,2,1,0:T(4,128)S(1)} %fusion.257, ...), kind=kLoop, calls=%fused_computation.16.clone.1 | loop fusion | flops 100335616 | bytes 3686400 | tf_op jit(solution)/shard_map/transpose(jvp(vmap()))/while/body/eval_jaxpr/checkpoint/reduce_sum | solution.py:56
  821.3 3.0 fusion.264
  826.6 15.5 %fusion.259 = f32[4,4,128,64]{2,1,3,0:T(4,128)S(1)} fusion(f32[4,4,128,64]{2,3,1,0:T(8,128)} %bitcast.498, f32[4,64,4,128]{3,1,2,0:T(8,128)} %copy-done.12, f32[4,64,4,128]{3,2,1,0:T(4,128)S(1)} %fusion.257, f32[4,64,64,4]{2,3,1,0:T(4,128)} %copy-done.14, pred[4,64,64]{2,1,0:T(8,128)(4,1)S(1)} %compare_and_fusion.5), kind=kLoop, calls=%fused_computation.11.clone.1 | loop fusion | flops 50200576 | bytes 2375680 | tf_op jit(solution)/shard_map/transpose(jvp(vmap()))/while
  842.1 12.5 fusion.258
  867.4 4.3 fusion.87
  872.1 4.2 fusion.86
  876.3 4.3 fusion.85
  880.6 4.4 fusion.84
  887.7 13.8 copy.349
  901.6 5.3 convolution_convert_fusion.1
  906.9 5.0 convolution_convert_fusion.2
  912.0 4.8 fusion.64
  916.7 8.0 pad_maximum_fusion
  924.8 21.2 %copy.351 = bf16[2048,4224]{1,0:T(8,128)(2,1)} copy(bf16[2048,4224]{0,1:T(8,128)(2,1)} %pad_maximum_fusion) | data formatting | bytes 34603008
  946.0 8.6 fusion.67
  954.6 5.0 all-to-all-start.4
  968.3 5.0 add_add_fusion
  973.3 99.9 %all-to-all-done.4 = f32[4,128,2048]{2,1,0:T(8,128)} async-done(((f32[4,128,2048]{2,1,0:T(8,128)}), f32[4,128,2048]{2,1,0:T(8,128)}, u32[]{:S(2)}, u32[]{:S(2)}) %all-to-all-start.4) | async-done | bytes 4194336 | tf_op jit(solution)/shard_map/all_to_all | solution.py:109
  1073.2 5.0 all-to-all-start.8
  1078.4 3.7 reduce_sum.223
  1083.7 51.5 %all-to-all-done.8 = f32[4,128,2048]{2,1,0:T(8,128)} async-done(((f32[4,128,2048]{2,1,0:T(8,128)}), f32[4,128,2048]{2,1,0:T(8,128)}, u32[]{:S(2)}, u32[]{:S(2)}) %all-to-all-start.8) | async-done | bytes 4194336 | tf_op jit(solution)/shard_map/all_to_all | solution.py:109
  1135.2 3.6 reduce_sum.228
  1141.3 8.1 all-to-all-start.9
  1149.5 3.4 fusion.128
  1152.9 8.7 all-to-all-done.9
  1167.6 222.1 %reduce-scatter.9.cloned.1.call-done = bf16[64,4224]{1,0:T(8,128)(2,1)} async-done(((bf16[2048,4224]{1,0:T(8,128)(2,1)}), bf16[64,4224]{1,0:T(8,128)(2,1)}) %reduce-scatter.9.cloned.1.call-update) | async-done | bytes 540688
  (374 shorter events, 149.5 us)
Async XLA Ops:
  7.2 33.6 %copy-start.7 = (bf16[1,1,128,2048]{3,2,1,0:T(8,128)(2,1)S(1)}, bf16[1,1,128,2048]{3,2,1,0:T(8,128)(2,1)}, u32[]{:S(2)}) copy-start(bf16[1,1,128,2048]{3,2,1,0:T(8,128)(2,1)} %param.18) | copy-start | bytes 1572868
  7.2 247.0 %all-gather.2.cloned.1.call-start = ((), (), s32[]{:S(2)}) async-start(), calls=%async_computation.12 | async-start | bytes 28655616 | tf_op jit(solution)/shard_map/all_gather | solution.py:160
  16.7 22.9 %all-to-all-start = ((f32[128,3,16]{2,1,0:T(4,128)}), f32[128,3,16]{2,1,0:T(4,128)S(1)}, u32[]{:S(2)}, u32[]{:S(2)}) async-start(f32[128,3,16]{2,1,0:T(4,128)} %broadcast_in_dim.179), calls=%async_computation | async-start | bytes 524288 | tf_op jit(solution)/shard_map/all_to_all | solution.py:116
  29.2 17.9 %copy-start.56 = (s32[1,4,128]{2,1,0:T(4,128)S(1)}, s32[1,4,128]{2,1,0:T(4,128)}, u32[]{:S(2)}) copy-start(s32[1,4,128]{2,1,0:T(4,128)} %param.19) | copy-start | bytes 6148
  29.7 17.4 %copy-start.54 = (f32[128]{0:T(128)}, f32[128]{0:T(128)S(1)}, u32[]{:S(2)}) copy-start(f32[128]{0:T(128)S(1)} %get-tuple-element.863) | copy-start | bytes 1540
  40.8 6.3 copy-start.45
  42.6 220.9 %all-to-all-start.1 = ((bf16[4,128,2048]{2,1,0:T(8,128)(2,1)}), bf16[4,128,2048]{2,1,0:T(8,128)(2,1)}, u32[]{:S(2)}, u32[]{:S(2)}) async-start(bf16[4,128,2048]{2,1,0:T(8,128)(2,1)} %broadcast_in_dim.180), calls=%async_computation.1 | async-start | bytes 4194304 | tf_op jit(solution)/shard_map/all_to_all | solution.py:102
  47.8 215.6 %copy-start.48 = (f32[4,128]{1,0:T(4,128)}, f32[4,128]{1,0:T(4,128)S(1)}, u32[]{:S(2)}) copy-start(f32[4,128]{1,0:T(4,128)S(1)} %get-tuple-element.828) | copy-start | bytes 6148
  47.9 215.6 %copy-start.50 = (f32[4,128]{1,0:T(4,128)}, f32[4,128]{1,0:T(4,128)S(1)}, u32[]{:S(2)}) copy-start(f32[4,128]{1,0:T(4,128)S(1)} %get-tuple-element.829) | copy-start | bytes 6148
  432.8 5.0 copy-start.39
  440.9 51.7 %copy-start.24 = (bf16[1,1,128,2048]{3,2,1,0:T(8,128)(2,1)S(1)}, bf16[1,1,128,2048]{3,2,1,0:T(8,128)(2,1)}, u32[]{:S(2)}) copy-start(bf16[1,1,128,2048]{3,2,1,0:T(8,128)(2,1)} %param.31) | copy-start | bytes 1572868
  492.6 6.2 copy-start.42
  494.2 7.3 copy-start.8
  494.2 30.3 %all-to-all-start.5 = ((bf16[4,128,2048]{2,1,0:T(8,128)(2,1)}), bf16[4,128,2048]{2,1,0:T(8,128)(2,1)}, u32[]{:S(2)}, u32[]{:S(2)}) async-start(bf16[4,128,2048]{2,1,0:T(8,128)(2,1)} %broadcast_in_dim.183), calls=%async_computation.5 | async-start | bytes 4194304 | tf_op jit(solution)/shard_map/all_to_all | solution.py:102
  498.9 149.2 %copy-start.43 = (f32[2048]{0:T(1024)}, f32[2048]{0:T(1024)S(1)}, u32[]{:S(2)}) copy-start(f32[2048]{0:T(1024)S(1)} %mul.610) | copy-start | bytes 24580
  501.5 146.6 %copy-start.5 = (f32[128,2048]{1,0:T(8,128)}, f32[128,2048]{1,0:T(8,128)S(1)}, u32[]{:S(2)}) copy-start(f32[128,2048]{1,0:T(8,128)S(1)} %reduce_sum.220) | copy-start | bytes 3145732
  501.7 146.4 %copy-start.52 = (f32[128]{0:T(128)}, f32[128]{0:T(128)S(1)}, u32[]{:S(2)}) copy-start(f32[128]{0:T(128)S(1)} %get-tuple-element.865) | copy-start | bytes 1540
  501.7 146.4 %copy-start.57 = (f32[128]{0:T(128)}, f32[128]{0:T(128)S(1)}, u32[]{:S(2)}) copy-start(f32[128]{0:T(128)S(1)} %get-tuple-element.864) | copy-start | bytes 1540
  526.1 39.2 %all-to-all-start.3 = ((bf16[4,128,2048]{2,1,0:T(8,128)(2,1)}), bf16[4,128,2048]{2,1,0:T(8,128)(2,1)}, u32[]{:S(2)}, u32[]{:S(2)}) async-start(bf16[4,128,2048]{2,1,0:T(8,128)(2,1)} %broadcast_in_dim.181), calls=%async_computation.3 | async-start | bytes 4194304 | tf_op jit(solution)/shard_map/all_to_all | solution.py:102
  565.3 6.6 copy-start.66
  580.8 6.6 copy-start.65
  580.8 6.6 copy-start.62
  650.1 29.3 %all-to-all-start.7 = ((bf16[4,128,2048]{2,1,0:T(8,128)(2,1)}), bf16[4,128,2048]{2,1,0:T(8,128)(2,1)S(1)}, u32[]{:S(2)}, u32[]{:S(2)}) async-start(bf16[4,128,2048]{2,1,0:T(8,128)(2,1)} %broadcast_in_dim.184), calls=%async_computation.7 | async-start | bytes 4194304 | tf_op jit(solution)/shard_map/all_to_all | solution.py:102
  653.7 508.6 %reduce-scatter.7.cloned.1.call-start = ((), (), s32[]{:S(2)}) async-start(), calls=%async_computation.13 | async-start | bytes 10813440
  679.4 5.3 copy-start.32
  684.7 5.5 copy-start.36
  691.8 8.5 copy-start.3
  700.7 30.5 %copy-start.14 = (f32[4,64,64,4]{2,3,1,0:T(4,128)}, f32[4,64,64,4]{2,3,1,0:T(4,128)S(1)}, u32[]{:S(2)}) copy-start(f32[4,64,64,4]{2,3,1,0:T(4,128)S(1)} %copy.480) | copy-start | bytes 786436 | tf_op jit(solution)/shard_map/transpose(jvp(vmap()))/while
  702.1 29.1 %copy-start.12 = (f32[4,64,4,128]{3,1,2,0:T(8,128)}, f32[4,64,4,128]{3,1,2,0:T(8,128)S(1)}, u32[]{:S(2)}) copy-start(f32[4,64,4,128]{3,1,2,0:T(8,128)S(1)} %copy.477) | copy-start | bytes 1572868 | tf_op jit(solution)/shard_map/transpose(jvp(vmap()))/while
  703.7 27.5 %copy-start.16 = (f32[4,4,128,64]{2,1,3,0:T(4,128)}, f32[4,4,128,64]{2,1,3,0:T(4,128)S(1)}, u32[]{:S(2)}) copy-start(f32[4,4,128,64]{2,1,3,0:T(4,128)S(1)} %copy.479) | copy-start | bytes 1572868 | tf_op jit(solution)/shard_map/transpose(jvp(vmap()))/while
  739.2 15.5 %copy-start.13 = (f32[4,64,4,128]{3,1,2,0:T(8,128)S(1)}, f32[4,64,4,128]{3,1,2,0:T(8,128)}, u32[]{:S(2)}) copy-start(f32[4,64,4,128]{3,1,2,0:T(8,128)} %copy-done.12) | copy-start | bytes 1572868 | tf_op jit(solution)/shard_map/transpose(jvp(vmap()))/while
  739.2 15.5 %copy-start.15 = (f32[4,64,64,4]{2,3,1,0:T(4,128)S(1)}, f32[4,64,64,4]{2,3,1,0:T(4,128)}, u32[]{:S(2)}) copy-start(f32[4,64,64,4]{2,3,1,0:T(4,128)} %copy-done.14) | copy-start | bytes 786436 | tf_op jit(solution)/shard_map/transpose(jvp(vmap()))/while
  739.2 15.5 %copy-start.17 = (f32[4,4,128,64]{2,1,3,0:T(4,128)S(1)}, f32[4,4,128,64]{2,1,3,0:T(4,128)}, u32[]{:S(2)}) copy-start(f32[4,4,128,64]{2,1,3,0:T(4,128)} %copy-done.16) | copy-start | bytes 1572868 | tf_op jit(solution)/shard_map/transpose(jvp(vmap()))/while
  754.8 12.5 copy-start.4
  754.8 12.5 copy-start.21
  754.8 12.5 copy-start.26
  777.9 9.8 copy-start.3
  788.0 30.5 %copy-start.14 = (f32[4,64,64,4]{2,3,1,0:T(4,128)}, f32[4,64,64,4]{2,3,1,0:T(4,128)S(1)}, u32[]{:S(2)}) copy-start(f32[4,64,64,4]{2,3,1,0:T(4,128)S(1)} %copy.480) | copy-start | bytes 786436 | tf_op jit(solution)/shard_map/transpose(jvp(vmap()))/while
  789.4 29.1 %copy-start.12 = (f32[4,64,4,128]{3,1,2,0:T(8,128)}, f32[4,64,4,128]{3,1,2,0:T(8,128)S(1)}, u32[]{:S(2)}) copy-start(f32[4,64,4,128]{3,1,2,0:T(8,128)S(1)} %copy.477) | copy-start | bytes 1572868 | tf_op jit(solution)/shard_map/transpose(jvp(vmap()))/while
  791.0 27.5 %copy-start.16 = (f32[4,4,128,64]{2,1,3,0:T(4,128)}, f32[4,4,128,64]{2,1,3,0:T(4,128)S(1)}, u32[]{:S(2)}) copy-start(f32[4,4,128,64]{2,1,3,0:T(4,128)S(1)} %copy.479) | copy-start | bytes 1572868 | tf_op jit(solution)/shard_map/transpose(jvp(vmap()))/while
  826.6 15.5 %copy-start.13 = (f32[4,64,4,128]{3,1,2,0:T(8,128)S(1)}, f32[4,64,4,128]{3,1,2,0:T(8,128)}, u32[]{:S(2)}) copy-start(f32[4,64,4,128]{3,1,2,0:T(8,128)} %copy-done.12) | copy-start | bytes 1572868 | tf_op jit(solution)/shard_map/transpose(jvp(vmap()))/while
  826.6 15.5 %copy-start.15 = (f32[4,64,64,4]{2,3,1,0:T(4,128)S(1)}, f32[4,64,64,4]{2,3,1,0:T(4,128)}, u32[]{:S(2)}) copy-start(f32[4,64,64,4]{2,3,1,0:T(4,128)} %copy-done.14) | copy-start | bytes 786436 | tf_op jit(solution)/shard_map/transpose(jvp(vmap()))/while
  826.6 15.5 %copy-start.17 = (f32[4,4,128,64]{2,1,3,0:T(4,128)S(1)}, f32[4,4,128,64]{2,1,3,0:T(4,128)}, u32[]{:S(2)}) copy-start(f32[4,4,128,64]{2,1,3,0:T(4,128)} %copy-done.16) | copy-start | bytes 1572868 | tf_op jit(solution)/shard_map/transpose(jvp(vmap()))/while
  842.1 12.5 copy-start.4
  842.1 12.5 copy-start.21
  842.1 12.5 copy-start.26
  901.6 488.2 %reduce-scatter.9.cloned.1.call-start = ((), (), s32[]{:S(2)}) async-start(), calls=%async_computation.14 | async-start | bytes 17842176
  901.6 5.3 copy-start.63
  906.9 5.0 copy-start.64
  954.6 118.7 %all-to-all-start.4 = ((f32[4,128,2048]{2,1,0:T(8,128)}), f32[4,128,2048]{2,1,0:T(8,128)}, u32[]{:S(2)}, u32[]{:S(2)}) async-start(f32[4,128,2048]{2,1,0:T(8,128)} %bitcast.511), calls=%async_computation.4 | async-start | bytes 8388608 | tf_op jit(solution)/shard_map/all_to_all | solution.py:109
  1073.2 5.0 copy-start.47
  1073.2 61.9 %all-to-all-start.8 = ((f32[4,128,2048]{2,1,0:T(8,128)}), f32[4,128,2048]{2,1,0:T(8,128)}, u32[]{:S(2)}, u32[]{:S(2)}) async-start(f32[4,128,2048]{2,1,0:T(8,128)} %bitcast.503), calls=%async_computation.8 | async-start | bytes 8388608 | tf_op jit(solution)/shard_map/all_to_all | solution.py:109
  1078.3 60.4 %copy-start.9 = (bf16[1,1,128,2048]{3,2,1,0:T(8,128)(2,1)S(1)}, bf16[1,1,128,2048]{3,2,1,0:T(8,128)(2,1)}, u32[]{:S(2)}) copy-start(bf16[1,1,128,2048]{3,2,1,0:T(8,128)(2,1)} %param.18) | copy-start | bytes 1572868
  1078.3 60.4 %copy-start.46 = (f32[2048]{0:T(1024)S(1)}, f32[2048]{0:T(1024)}, u32[]{:S(2)}) copy-start(f32[2048]{0:T(1024)} %copy-done.45) | copy-start | bytes 24580
  1078.4 60.4 %copy-start.55 = (f32[128]{0:T(128)S(1)}, f32[128]{0:T(128)}, u32[]{:S(2)}) copy-start(f32[128]{0:T(128)} %copy-done.54) | copy-start | bytes 1540
  1082.1 67.4 %copy-start.6 = (f32[128,2048]{1,0:T(8,128)S(1)}, f32[128,2048]{1,0:T(8,128)}, u32[]{:S(2)}) copy-start(f32[128,2048]{1,0:T(8,128)} %copy-done.5) | copy-start | bytes 3145732
  1082.1 67.4 %copy-start.11 = (f32[128,2048]{1,0:T(8,128)S(1)}, f32[128,2048]{1,0:T(8,128)}, u32[]{:S(2)}) copy-start(f32[128,2048]{1,0:T(8,128)} %copy-done.10) | copy-start | bytes 3145732
  1082.1 67.4 %copy-start.25 = (bf16[1,1,128,2048]{3,2,1,0:T(8,128)(2,1)S(1)}, bf16[1,1,128,2048]{3,2,1,0:T(8,128)(2,1)}, u32[]{:S(2)}) copy-start(bf16[1,1,128,2048]{3,2,1,0:T(8,128)(2,1)} %param.31) | copy-start | bytes 1572868
  1082.1 67.4 %copy-start.44 = (f32[2048]{0:T(1024)S(1)}, f32[2048]{0:T(1024)}, u32[]{:S(2)}) copy-start(f32[2048]{0:T(1024)} %copy-done.43) | copy-start | bytes 24580
  1082.1 67.4 %copy-start.53 = (f32[128]{0:T(128)S(1)}, f32[128]{0:T(128)}, u32[]{:S(2)}) copy-start(f32[128]{0:T(128)} %copy-done.52) | copy-start | bytes 1540
  1082.1 67.4 %copy-start.58 = (f32[128]{0:T(128)S(1)}, f32[128]{0:T(128)}, u32[]{:S(2)}) copy-start(f32[128]{0:T(128)} %copy-done.57) | copy-start | bytes 1540
  1082.1 67.4 %copy-start.60 = (f32[128]{0:T(128)S(1)}, f32[128]{0:T(128)}, u32[]{:S(2)}) copy-start(f32[128]{0:T(128)} %copy-done.59) | copy-start | bytes 1540
  1082.1 67.4 %copy-start.61 = (f32[128]{0:T(128)S(1)}, f32[128]{0:T(128)}, u32[]{:S(2)}) copy-start(f32[128]{0:T(128)} %get-tuple-element.862) | copy-start | bytes 1540
  1141.3 20.3 %all-to-all-start.9 = ((f32[128,3,16]{2,1,0:T(4,128)}), f32[128,3,16]{2,1,0:T(4,128)S(1)}, u32[]{:S(2)}, u32[]{:S(2)}) async-start(f32[128,3,16]{2,1,0:T(4,128)} %copy.307), calls=%async_computation.9 | async-start | bytes 524288 | tf_op jit(solution)/shard_map/all_to_all | solution.py:123
  (33 other events, 84.9 us)
Sparse Core Ops, SparseCore 0:
  15.4 238.7 all-gather.1
  901.7 205.9 reduce-scatter.6
  1113.5 276.2 reduce-scatter.8
